TPU v7x, 32 devices: a whole 2x2x4 slice. The times are simulated.
32 devices in a mesh: ctx: 8 (over z, y), grp: 4 (over x, core).
Axes of the slice: x: 2, y: 2, z: 4, core: 2. Of those that a mesh axis runs over, the one named last changes fastest.
Arguments:
- channels: bfloat16 [4096, 5120], P(('ctx', 'grp')), may hold values from -6 to 6
- gates: bfloat16 [4096, 5120], P(('ctx', 'grp')), may hold values from -6 to 6
- b_proj: bfloat16 [4096, 128], P(('ctx', 'grp')), may hold values from -6 to 6
- c_proj: bfloat16 [4096, 128], P(('ctx', 'grp')), may hold values from -0.5 to 0.5
- step_size: bfloat16 [4096, 80], P(('ctx', 'grp')), may hold values from 0.001 to 1, as said below
- log_decay: bfloat16 [4096, 80], P(('ctx', 'grp')), may hold values from -1 to 0, as said below
- skip_gain: float32 [80], P('grp'), may hold values from 0.5 to 2
- norm_gain: float32 [5120], P('grp'), may hold values from 0.1 to 1.9
- out_weight: bfloat16 [5120, 2560], P('grp'), may hold values from -0.078125 to 0.078125
Outputs:
- layer_out: bfloat16 [4096, 2560], P(('ctx', 'grp'))
Inputs may be any that keep to these rules, and one draw needn't show every extreme that they name: `step_size`: each token's step of each head is positive. `log_decay`: each token's log decay of each head is negative.
All inputs are finite; a program needn't handle non-finite values.
Results may differ from a plain program's by a relative error of at most 0.009.
Values may be sent and summed in bfloat16 or wider, within the bound.
A program may use at most 128 MiB of HBM per device.

v0:
```python
import jax
import jax.numpy as jnp
from jax import lax
from jax.sharding import PartitionSpec as P

HEADS = 80
HD = 64
NSTATE = 128
GROUP = 256


def prefix_2(value, axis, join, neutral):
    count, mine = (lax.axis_size(axis), lax.axis_index(axis))
    pieces = jax.tree.map(lambda part: lax.all_gather(part, axis), value)
    so_far = jax.tree.map(
        lambda part, zero: jnp.full_like(part, 0) + jnp.asarray(zero, part.dtype), value, neutral
    )

    def turn(position, so_far):
        longer = join(so_far, jax.tree.map(lambda part: part[position], pieces))
        return jax.tree.map(lambda new, old: jnp.where(position < mine, new, old), longer, so_far)

    return lax.fori_loop(0, count - 1, turn, so_far)


def local_scan(chan_heads, step_heads, decay_heads, b_rows, c_rows):
    highest = lax.Precision.HIGHEST
    piece_len = chan_heads.shape[0]
    nheads = step_heads.shape[1]
    blocks = piece_len // GROUP
    running = jnp.cumsum(decay_heads.astype(jnp.float32).reshape(blocks, GROUP, nheads), axis=1)
    running_t = jnp.transpose(running, (0, 2, 1))
    chan_f = chan_heads.astype(jnp.float32).reshape(piece_len, nheads, HD)
    inputs = (chan_f * step_heads.astype(jnp.float32)[:, :, None]).reshape(
        blocks, GROUP, nheads, HD
    )
    b_blocks = b_rows.reshape(blocks, GROUP, NSTATE)
    c_blocks = c_rows.reshape(blocks, GROUP, NSTATE)
    scores = jnp.einsum("qin,qjn->qij", c_blocks, b_blocks, preferred_element_type=jnp.float32)
    rows_at = lax.broadcasted_iota(jnp.int32, (GROUP, GROUP), 0)
    cols_at = lax.broadcasted_iota(jnp.int32, (GROUP, GROUP), 1)
    causal = rows_at >= cols_at
    spread = running_t[:, :, :, None] - running_t[:, :, None, :]
    weights = jnp.where(causal[None, None], jnp.exp(spread), 0.0) * scores[:, None]
    y_intra = jnp.einsum("qhij,qjhp->qihp", weights, inputs, precision=highest)
    tail_decay = jnp.exp(running[:, -1:, :] - running)
    b_float = b_blocks.astype(jnp.float32)
    c_float = c_blocks.astype(jnp.float32)
    group_states = jnp.einsum(
        "qjhp,qjn->qhpn", inputs * tail_decay[..., None], b_float, precision=highest
    )
    totals = jnp.exp(running[:, -1, :])

    def carry_step(carried, packed):
        factor, fresh_state = packed
        return (factor[:, None, None] * carried + fresh_state, carried)

    final_state, starts = lax.scan(
        carry_step, jnp.zeros((nheads, HD, NSTATE), jnp.float32), (totals, group_states)
    )
    y_inter = (
        jnp.einsum("qin,qhpn->qihp", c_float, starts, precision=highest)
        * jnp.exp(running)[..., None]
    )
    group_logs = running[:, -1, :]
    offsets = jnp.cumsum(group_logs, axis=0) - group_logs
    piece_cum = (running + offsets[:, None, :]).reshape(piece_len, nheads)
    piece_log = jnp.sum(group_logs, axis=0)
    local_out = (y_intra + y_inter).reshape(piece_len, nheads, HD)
    return (local_out, final_state, piece_log, piece_cum, chan_f)


def local(channels, gates, b_proj, c_proj, step_size, log_decay, skip_gain, norm_gain, out_weight):
    highest = lax.Precision.HIGHEST
    chan_heads, gate_heads, step_heads, decay_heads = (
        lax.all_to_all(channels, "grp", split_axis=1, concat_axis=0, tiled=True),
        lax.all_to_all(gates, "grp", split_axis=1, concat_axis=0, tiled=True),
        lax.all_to_all(step_size, "grp", split_axis=1, concat_axis=0, tiled=True),
        lax.all_to_all(log_decay, "grp", split_axis=1, concat_axis=0, tiled=True),
    )
    b_rows, c_rows = (
        lax.all_gather(b_proj, "grp", axis=0, tiled=True),
        lax.all_gather(c_proj, "grp", axis=0, tiled=True),
    )
    local_out, final_state, piece_log, piece_cum, chan_f = local_scan(
        chan_heads, step_heads, decay_heads, b_rows, c_rows
    )
    piece_factor = jnp.exp(piece_log)

    def combine(early_part, later_part):
        return (
            early_part[0] * later_part[0],
            later_part[0][:, None, None] * early_part[1] + later_part[1],
        )

    identity = (jnp.ones_like(piece_factor), jnp.zeros_like(final_state))
    prefix = prefix_2((piece_factor, final_state), "ctx", combine, identity)
    incoming = prefix[1]
    correction = jnp.einsum("tn,hpn->thp", c_rows.astype(jnp.float32), incoming, precision=highest)
    correction = correction * jnp.exp(piece_cum)[:, :, None]
    ssm_out = local_out + correction + skip_gain[None, :, None] * chan_f
    piece_len = chan_heads.shape[0]
    gated_out = ssm_out.reshape(piece_len, chan_heads.shape[1]) * jax.nn.silu(
        gate_heads.astype(jnp.float32)
    )
    row_squares = lax.psum(jnp.sum(gated_out * gated_out, axis=1), "grp")
    scale = lax.rsqrt(row_squares / (HEADS * HD) + 1e-05)
    normed = (gated_out * scale[:, None] * norm_gain[None, :]).astype(jnp.bfloat16)
    return lax.psum_scatter(
        jnp.dot(normed, out_weight, preferred_element_type=jnp.float32).astype(jnp.bfloat16),
        "grp",
        scatter_dimension=0,
        tiled=True,
    )


def solution(mesh):
    in_specs = (
        P(("ctx", "grp"), None),
        P(("ctx", "grp"), None),
        P(("ctx", "grp"), None),
        P(("ctx", "grp"), None),
        P(("ctx", "grp"), None),
        P(("ctx", "grp"), None),
        P("grp"),
        P("grp"),
        P("grp", None),
    )
    out_specs = P(("ctx", "grp"), None)
    return jax.shard_map(local, mesh=mesh, in_specs=in_specs, out_specs=out_specs, check_vma=False)
```

profile of v0, /device:TPU:0, one launch (start us, length us, event | category | flops | bytes accessed | tf_op | source)
XLA Modules:
  0.0 233.1 jit_solution(6459703165636211416)
XLA Ops:
  6.5 1.4 all_to_all.44
  7.9 4.2 %all-to-all-start.2 = ((bf16[128,4,20]{0,2,1:T(8,128)(2,1)}), bf16[128,4,20]{0,2,1:T(8,128)(2,1)S(1)}, u32[]{:S(2)}, u32[]{:S(2)}) async-start(bf16[128,4,20]{0,2,1:T(8,128)(2,1)} %all_to_all.44), calls=%async_computation.2 | async-start | bytes 49152 | tf_op jit(solution)/shard_map/all_to_all | solution.py:79
  12.1 5.8 %all_gather.17 = bf16[512,128]{1,0:T(8,128)(2,1)S(1)} all-gather(bf16[128,128]{1,0:T(8,128)(2,1)} %param.15), channel_id=1, replica_groups=mesh['ctx'=8,'grp'=4] {'grp'}, dimensions={0}, use_global_device_ids=true | all-gather | bytes 163840 | tf_op jit(solution)/shard_map/all_gather | solution.py:82
  17.9 2.4 %copy.51 = bf16[128,5120]{0,1:T(8,128)(2,1)} copy(bf16[128,5120]{1,0:T(8,128)(2,1)} %param.13) | data formatting | bytes 2621440 | tf_op args[0]
  20.3 0.6 all_to_all.42
  20.9 3.3 %all-to-all-start.1 = ((bf16[128,4,20]{0,2,1:T(8,128)(2,1)}), bf16[128,4,20]{0,2,1:T(8,128)(2,1)S(1)}, u32[]{:S(2)}, u32[]{:S(2)}) async-start(bf16[128,4,20]{0,2,1:T(8,128)(2,1)} %all_to_all.42), calls=%async_computation.1 | async-start | bytes 49152 | tf_op jit(solution)/shard_map/all_to_all | solution.py:78
  24.3 1.2 reduce-window.6
  25.5 0.2 slice_reduce_fusion
  25.7 2.3 %all-to-all-done.1 = bf16[128,4,20]{0,2,1:T(8,128)(2,1)S(1)} async-done(((bf16[128,4,20]{0,2,1:T(8,128)(2,1)}), bf16[128,4,20]{0,2,1:T(8,128)(2,1)S(1)}, u32[]{:S(2)}, u32[]{:S(2)}) %all-to-all-start.1) | async-done | bytes 20512 | tf_op jit(solution)/shard_map/all_to_all | solution.py:78
  28.1 3.5 %all-to-all-start = ((bf16[128,4,1280]{0,2,1:T(8,128)(2,1)}), bf16[128,4,1280]{0,2,1:T(8,128)(2,1)S(1)}, u32[]{:S(2)}, u32[]{:S(2)}) async-start(bf16[128,4,1280]{0,2,1:T(8,128)(2,1)} %bitcast), calls=%async_computation | async-start | bytes 2621440 | tf_op jit(solution)/shard_map/all_to_all | solution.py:76
  32.0 0.1 copy.60
  32.1 0.3 slice_subtract_fusion
  32.4 0.1 copy.65
  32.5 0.1 copy.66
  32.6 0.1 copy.61
  32.8 0.7 exponential_bitcast_fusion
  33.5 15.3 %all-to-all-done = bf16[128,4,1280]{0,2,1:T(8,128)(2,1)S(1)} async-done(((bf16[128,4,1280]{0,2,1:T(8,128)(2,1)}), bf16[128,4,1280]{0,2,1:T(8,128)(2,1)S(1)}, u32[]{:S(2)}, u32[]{:S(2)}) %all-to-all-start) | async-done | bytes 1310752 | tf_op jit(solution)/shard_map/all_to_all | solution.py:76
  48.8 0.2 convert_bitcast_fusion.1
  49.0 5.4 %copy.52 = f32[4,128,1280]{1,0,2:T(4,128)S(1)} copy(f32[4,128,1280]{1,2,0:T(8,128)S(1)} %convert_bitcast_fusion.1) | data formatting | bytes 5242880 | tf_op jit(solution)/shard_map/convert_element_type | solution.py:33
  54.5 3.3 %reshape.122 = f32[2,256,20,64]{1,0,3,2:T(2,128)} reshape(f32[4,128,1280]{1,0,2:T(4,128)S(1)} %copy.52) | data formatting | bytes 5242880 | tf_op jit(solution)/shard_map/convert_element_type | solution.py:33
  57.8 5.1 %broadcast_multiply_fusion = (f32[2,256,20,64]{1,0,3,2:T(2,128)S(1)}, f32[2,256,20,64]{1,0,3,2:T(2,128)}) fusion(f32[2,256,20]{1,0,2:T(2,128)S(1)} %get-tuple-element.189, f32[2,256,20,64]{1,0,3,2:T(2,128)} %reshape.122, f32[2,256,20]{1,0,2:T(2,128)S(1)} %reshape.123), kind=kLoop, calls=%fused_computation.39 | loop fusion | flops 1310720 | bytes 7946240 | tf_op jit(solution)/shard_map/mul | solution.py:50
  62.9 2.4 %fusion.22 = f32[2,20,64,128]{3,2,1,0:T(8,128)} fusion(bf16[2,256,128,1]{2,1,3,0:T(8,128)(2,1)S(1)} %bitcast.131, f32[2,256,20,64]{1,0,3,2:T(2,128)S(1)} %get-tuple-element.186), kind=kOutput, calls=%fused_computation.33 | convolution fusion | flops 1006632960 | bytes 4063232 | tf_op jit(solution)/shard_map/qjhp,qjn->qhpn/dot_general | solution.py:49
  65.3 4.3 %while.27 = (s32[]{:T(128)}, f32[20,64,128]{2,1,0:T(8,128)S(1)}, f32[2,20,64,128]{3,2,1,0:T(8,128)}, f32[2,20]{1,0:T(2,128)S(1)}, f32[2,20,64,128]{3,2,1,0:T(8,128)}, /*index=5*/s32[]{:T(128)}, s32[]{:T(128)}) while((s32[]{:T(128)}, f32[20,64,128]{2,1,0:T(8,128)S(1)}, f32[2,20,64,128]{3,2,1,0:T(8,128)}, f32[2,20]{1,0:T(2,128)S(1)}, ...), condition=%wide.region_3.4_spmd.clone, body=%wide.region_2.3_spmd.clone.sunk | while | flops 655363 | bytes 3277648 | solution.py:58
  65.3 0.9 bitcast_dynamic-update-slice_fusion.2
  66.2 1.2 bitcast_add_fusion.3
  67.5 0.9 bitcast_dynamic-update-slice_fusion.2
  68.4 1.2 bitcast_add_fusion.3
  69.6 0.8 copy-done
  70.5 2.5 %copy.68 = bf16[128,5120]{0,1:T(8,128)(2,1)} copy(bf16[128,5120]{1,0:T(8,128)(2,1)} %param.14) | data formatting | bytes 2621440 | tf_op args[1]
  72.9 4.3 %all-to-all-start.3 = ((bf16[128,4,1280]{0,2,1:T(8,128)(2,1)}), bf16[128,4,1280]{0,2,1:T(8,128)(2,1)}, u32[]{:S(2)}, u32[]{:S(2)}) async-start(bf16[128,4,1280]{0,2,1:T(8,128)(2,1)} %bitcast.127), calls=%async_computation.3 | async-start | bytes 2621440 | tf_op jit(solution)/shard_map/all_to_all | solution.py:77
  77.4 0.6 dynamic-slice
  78.5 17.5 %all_gather.16 = bf16[512,128]{1,0:T(8,128)(2,1)S(1)} all-gather(bf16[128,128]{1,0:T(8,128)(2,1)} %param.16), channel_id=1, replica_groups=mesh['ctx'=8,'grp'=4] {'grp'}, dimensions={0}, use_global_device_ids=true | all-gather | bytes 163840 | tf_op jit(solution)/shard_map/all_gather | solution.py:83
  96.0 0.6 iota_compare_fusion
  96.7 1.0 fusion.28
  97.7 1.4 copy.57
  99.1 0.8 copy.63
  99.9 0.1 exponential_dynamic-update-slice_fusion
  100.0 22.7 %all-reduce = f32[160]{0:T(256)S(1)} all-reduce(f32[160]{0:T(256)S(1)} %exponential_dynamic-update-slice_fusion), channel_id=2, replica_groups=mesh['ctx'=8,'grp'=4] {'ctx'}, use_global_device_ids=true, to_apply=%add | all-reduce | flops 160 | bytes 1280
  122.7 0.1 reshape.129
  122.8 0.8 pad
  123.6 0.6 copy.75
  124.2 2.1 reshape.125
  126.3 13.1 %fusion.2 = f32[2,20,64,256]{3,2,1,0:T(8,128)S(1)} fusion(f32[2,256,256]{2,1,0:T(8,128)} %fusion.28, f32[2,20,256]{2,1,0:T(8,128)} %copy.57, pred[256,256]{1,0:T(8,128)(4,1)S(1)} %copy-done.3, f32[2,256,20,64]{1,0,3,2:T(2,128)} %get-tuple-element.187), kind=kOutput, calls=%fused_computation.7 | convolution fusion | flops 2021130240 | bytes 5873664 | tf_op jit(solution)/shard_map/qhij,qjhp->qihp/dot_general | solution.py:45
  139.5 1.3 fusion.21
  140.9 1.9 copy.74
  142.7 1.6 copy.69
  144.3 1.7 convert_bitcast_fusion
  146.1 4.1 %copy.71 = f32[4,128,1280]{1,0,2:T(4,128)} copy(f32[4,128,1280]{2,1,0:T(8,128)} %convert_bitcast_fusion) | data formatting | bytes 5242880 | tf_op jit(solution)/shard_map/convert_element_type | solution.py:104
  150.2 4.1 %reshape.127 = f32[512,20,64]{0,2,1:T(8,128)} reshape(f32[4,128,1280]{1,0,2:T(4,128)} %copy.71) | data formatting | bytes 5242880 | tf_op jit(solution)/shard_map/convert_element_type | solution.py:104
  154.4 3.5 %all-gather.4.cloned.1.call-done = f32[160,64,128]{2,1,0:T(8,128)} async-done(((f32[20,64,128]{2,1,0:T(8,128)}), f32[160,64,128]{2,1,0:T(8,128)}) %all-gather.4.cloned.1.call-update) | async-done | bytes 5242896 | tf_op jit(solution)/shard_map/all_gather | solution.py:14
  157.9 8.9 %while.28 = (s32[]{:T(128)}, f32[20,64,128]{2,1,0:T(8,128)S(1)}, s32[]{:T(128)}, f32[8,20]{1,0:T(8,128)S(1)}, f32[8,20,64,128]{3,2,1,0:T(8,128)}, /*index=5*/s32[]{:T(128)}, s32[]{:T(128)}) while((s32[]{:T(128)}, f32[20,64,128]{2,1,0:T(8,128)S(1)}, s32[]{:T(128)}, f32[8,20]{1,0:T(8,128)S(1)}, f32[8,20,64,128]{3,2,1,0:T(8,128)}, ...), condition=%wide.region_6.7_spmd.clone, body=%wide.region_5.6_spmd.clone.sunk | while | flops 655364 | bytes 1966425 | solution.py:23
  157.9 1.2 fusion.40
  159.2 1.2 fusion.40
  160.5 1.2 fusion.40
  161.7 1.2 fusion.40
  163.0 1.2 fusion.40
  164.3 1.2 fusion.40
  165.6 1.2 fusion.40
  166.8 6.9 %multiply_reduce_fusion = (f32[512]{0:T(512)S(1)}, f32[512,20,64]{0,2,1:T(8,128)}) fusion(f32[512,20,64]{0,2,1:T(8,128)} %reshape.127, f32[512,20,64]{0,2,1:T(8,128)} %reshape.125, f32[20]{0:T(128)S(1)} %copy-done.7, f32[512,20,64]{0,2,1:T(8,128)} %bitcast.128, f32[512,20]{0,1:T(8,128)S(1)} %bitcast.139, f32[20,64,128]{2,1,0:T(8,128)S(1)} %get-tuple-element.129, ...), kind=kOutput, calls=%fused_computation.37 | convolution fusion | flops 1013841408 | bytes 11315280 | tf_op jit(solution)/shard_map/tn,hpn->thp/dot_general | solution.py:99
  173.7 3.2 %copy.70 = f32[512,1280]{1,0:T(8,128)} copy(f32[512,1280]{0,1:T(8,128)} %bitcast.129) | data formatting | bytes 5242880 | tf_op jit(solution)/shard_map/reshape | solution.py:103
  176.9 5.9 %psum.7 = f32[512]{0:T(512)S(1)} all-reduce(f32[512]{0:T(512)S(1)} %get-tuple-element.193), channel_id=1, replica_groups=mesh['ctx'=8,'grp'=4] {'grp'}, use_global_device_ids=true, to_apply=%region_9.10 | all-reduce | flops 512 | bytes 4096 | tf_op jit(solution)/shard_map/psum | solution.py:106
  182.9 2.6 %fusion.25 = bf16[512,1280]{1,0:T(8,128)(2,1)S(1)} fusion(f32[512,1280]{1,0:T(8,128)} %copy.70, bf16[128,4,1280]{2,0,1:T(8,128)(2,1)S(1)} %copy.69, f32[1280]{0:T(1024)S(1)} %copy-done.6, f32[512]{0:T(512)S(1)} %add_rsqrt_fusion), kind=kLoop, calls=%fused_computation.38 | loop fusion | flops 5898240 | bytes 5250048 | tf_op jit(solution)/shard_map/convert_element_type | solution.py:108
  185.5 7.7 %convolution_convert_fusion = bf16[512,2560]{1,0:T(8,128)(2,1)} fusion(bf16[512,1280]{1,0:T(8,128)(2,1)S(1)} %fusion.25, bf16[1280,2560]{1,0:T(8,128)(2,1)} %param.21), kind=kOutput, calls=%fused_computation.17 | convolution fusion | flops 3356753920 | bytes 10485760 | tf_op jit(solution)/shard_map/dot_general | solution.py:110
  193.2 33.1 %reduce-scatter.2.cloned.1.call-done = bf16[128,2560]{1,0:T(8,128)(2,1)} async-done(((bf16[512,2560]{1,0:T(8,128)(2,1)}), bf16[128,2560]{1,0:T(8,128)(2,1)}) %reduce-scatter.2.cloned.1.call-update) | async-done | bytes 655376 | tf_op jit(solution)/shard_map/reduce_scatter | solution.py:109
  (53 shorter events, 0.7 us)
Async XLA Ops:
  6.5 13.8 %copy-start.5 = (bf16[128,80]{0,1:T(8,128)(2,1)S(1)}, bf16[128,80]{0,1:T(8,128)(2,1)}, u32[]{:S(2)}) copy-start(bf16[128,80]{0,1:T(8,128)(2,1)} %param.17) | copy-start | bytes 61444
  7.9 13.0 %all-to-all-start.2 = ((bf16[128,4,20]{0,2,1:T(8,128)(2,1)}), bf16[128,4,20]{0,2,1:T(8,128)(2,1)S(1)}, u32[]{:S(2)}, u32[]{:S(2)}) async-start(bf16[128,4,20]{0,2,1:T(8,128)(2,1)} %all_to_all.44), calls=%async_computation.2 | async-start | bytes 49152 | tf_op jit(solution)/shard_map/all_to_all | solution.py:79
  20.9 7.1 %all-to-all-start.1 = ((bf16[128,4,20]{0,2,1:T(8,128)(2,1)}), bf16[128,4,20]{0,2,1:T(8,128)(2,1)S(1)}, u32[]{:S(2)}, u32[]{:S(2)}) async-start(bf16[128,4,20]{0,2,1:T(8,128)(2,1)} %all_to_all.42), calls=%async_computation.1 | async-start | bytes 49152 | tf_op jit(solution)/shard_map/all_to_all | solution.py:78
  28.1 20.8 %all-to-all-start = ((bf16[128,4,1280]{0,2,1:T(8,128)(2,1)}), bf16[128,4,1280]{0,2,1:T(8,128)(2,1)S(1)}, u32[]{:S(2)}, u32[]{:S(2)}) async-start(bf16[128,4,1280]{0,2,1:T(8,128)(2,1)} %bitcast), calls=%async_computation | async-start | bytes 2621440 | tf_op jit(solution)/shard_map/all_to_all | solution.py:76
  31.6 126.3 %all-gather.4.cloned.1.call-start = ((), (), s32[]{:S(2)}) async-start(), calls=%async_computation.6 | async-start | bytes 5898240 | tf_op jit(solution)/shard_map/all_gather | solution.py:14
  31.8 17.0 %copy-start.2 = (f32[2,20,256]{2,0,1:T(2,128)}, f32[2,20,256]{2,0,1:T(2,128)S(1)}, u32[]{:S(2)}) copy-start(f32[2,20,256]{2,0,1:T(2,128)S(1)} %reduce_window_sum.35) | copy-start | bytes 122884
  69.6 0.8 copy-start
  70.5 6.9 %copy-start.8 = (u32[32]{0:T(128)S(1)}, u32[32]{0:T(128)}, u32[]{:S(2)}) copy-start(u32[32]{0:T(128)} %constant.61) | copy-start | bytes 388
  72.9 69.8 %all-to-all-start.3 = ((bf16[128,4,1280]{0,2,1:T(8,128)(2,1)}), bf16[128,4,1280]{0,2,1:T(8,128)(2,1)}, u32[]{:S(2)}, u32[]{:S(2)}) async-start(bf16[128,4,1280]{0,2,1:T(8,128)(2,1)} %bitcast.127), calls=%async_computation.3 | async-start | bytes 2621440 | tf_op jit(solution)/shard_map/all_to_all | solution.py:77
  77.3 149.0 %reduce-scatter.2.cloned.1.call-start = ((), (), s32[]{:S(2)}) async-start(), calls=%async_computation.5 | async-start | bytes 3276800 | tf_op jit(solution)/shard_map/reduce_scatter | solution.py:109
  124.2 2.1 copy-start.3
  126.3 13.1 %copy-start.1 = (f32[2,20,64,128]{3,2,1,0:T(8,128)S(1)}, f32[2,20,64,128]{3,2,1,0:T(8,128)}, u32[]{:S(2)}) copy-start(f32[2,20,64,128]{3,2,1,0:T(8,128)} %get-tuple-element.127) | copy-start | bytes 3932164
  157.9 8.9 %copy-start.4 = (f32[3,8,2,256]{3,1,2,0:T(8,128)S(1)}, f32[3,8,2,256]{3,1,2,0:T(8,128)}, u32[]{:S(2)}) copy-start(f32[3,8,2,256]{3,1,2,0:T(8,128)} %copy.75) | copy-start | bytes 147460
  157.9 8.9 %copy-start.7 = (f32[20]{0:T(128)S(1)}, f32[20]{0:T(128)}, u32[]{:S(2)}) copy-start(f32[20]{0:T(128)} %param.19) | copy-start | bytes 244
  173.7 9.2 %copy-start.6 = (f32[1280]{0:T(1024)S(1)}, f32[1280]{0:T(1024)}, u32[]{:S(2)}) copy-start(f32[1280]{0:T(1024)} %param.20) | copy-start | bytes 15364
Sparse Core Ops, SparseCore 0:
  70.6 87.2 all-gather.3
  193.3 32.9 reduce-scatter.1
where the time goes:
time: 235 us; the launch traced here: 233 us
  waiting for transfers between devices  54.3 us (23%)
  blocking collectives  51.9 us (22%)
  local copies, waits for them, and re-layouts  38.9 us (17%)
  matrix products  32.5 us (14%)
  other arithmetic  25.6 us (11%)
  starting transfers between devices  15.4 us (7%)
  between operations  14.3 us (6%)
    reduce_scatter x1, waiting for transfers between devices, local(): lax.psum_scatter(jnp.dot(normed, out_weight, preferred_element_type=jnp.f...  33.1 us
    unnamed x1, blocking collectives  22.7 us
    all_gather x1, blocking collectives, local(): lax.all_gather(c_proj, 'grp', axis=0, tiled=True)  17.5 us
    all_to_all x1, waiting for transfers between devices, local(): lax.all_to_all(channels, 'grp', split_axis=1, concat_axis=0, tiled=True)  15.3 us
    dot_general x1, matrix products, local_scan(): y_intra = jnp.einsum('qhij,qjhp->qihp', weights, inputs, precision=highest)  13.1 us
    convert_element_type x3, local copies, waits for them, and re-layouts, local_scan(): chan_f = chan_heads.astype(jnp.float32).reshape(piece_len, nheads, HD)  10.9 us
    select_n x7, other arithmetic, turn(): jnp.where(position < mine, new, old)  8.64 us
    convert_element_type x2, local copies, waits for them, and re-layouts, local(): gate_heads.astype(jnp.float32)  8.27 us
  transfers between devices with their start and end apart: 6, of which 4 were waited for; matrix products, arithmetic and copies ran while one was open for 19% of the time, Pallas kernels for 0%

commit v1 on v0

--- a/solution.py
+++ b/solution.py
@@ -103,7 +103,7 @@
     gated_out = ssm_out.reshape(piece_len, chan_heads.shape[1]) * jax.nn.silu(
         gate_heads.astype(jnp.float32)
     )
-    row_squares = lax.psum(jnp.sum(gated_out * gated_out, axis=1), "grp")
+    row_squares = jnp.sum(lax.all_gather(jnp.sum(gated_out * gated_out, axis=1), "grp"), axis=0)
     scale = lax.rsqrt(row_squares / (HEADS * HD) + 1e-05)
     normed = (gated_out * scale[:, None] * norm_gain[None, :]).astype(jnp.bfloat16)
     return lax.psum_scatter(

time: 235 us -> 234 us (level)
    psum x1 -> x0, blocking collectives: 5.91 us -> none  [local(): row_squares = lax.psum(jnp.sum(gated_out * gated_out, axis=1), 'grp')]
    all_gather x0 -> x1, blocking collectives: none -> 5.37 us  [local(): lax.all_gather(jnp.sum(gated_out * gated_out, axis=1), 'grp')]
where the time goes in v1:
time: 234 us; the launch traced here: 233 us
  waiting for transfers between devices  54.3 us (23%)
  blocking collectives  51.4 us (22%)
  local copies, waits for them, and re-layouts  38.9 us (17%)
  matrix products  32.5 us (14%)
  other arithmetic  25.6 us (11%)
  starting transfers between devices  15.4 us (7%)
  between operations  14.3 us (6%)
    reduce_scatter x1, waiting for transfers between devices, local(): lax.psum_scatter(jnp.dot(normed, out_weight, preferred_element_type=jnp.f...  33 us
    unnamed x1, blocking collectives  22.7 us
    all_gather x1, blocking collectives, local(): lax.all_gather(c_proj, 'grp', axis=0, tiled=True)  17.5 us
    all_to_all x1, waiting for transfers between devices, local(): lax.all_to_all(channels, 'grp', split_axis=1, concat_axis=0, tiled=True)  15.3 us
    dot_general x1, matrix products, local_scan(): y_intra = jnp.einsum('qhij,qjhp->qihp', weights, inputs, precision=highest)  13.1 us
    convert_element_type x3, local copies, waits for them, and re-layouts, local_scan(): chan_f = chan_heads.astype(jnp.float32).reshape(piece_len, nheads, HD)  10.9 us
    select_n x7, other arithmetic, turn(): jnp.where(position < mine, new, old)  8.64 us
    convert_element_type x2, local copies, waits for them, and re-layouts, local(): gate_heads.astype(jnp.float32)  8.27 us
  transfers between devices with their start and end apart: 6, of which 4 were waited for; matrix products, arithmetic and copies ran while one was open for 19% of the time, Pallas kernels for 0%

profile of v1, /device:TPU:0, one launch (start us, length us, event | category | flops | bytes accessed | tf_op | source)
XLA Modules:
  0.0 232.6 jit_solution(11473839349569721858)
XLA Ops:
  6.5 1.4 all_to_all.44
  7.9 4.2 %all-to-all-start.2 = ((bf16[128,4,20]{0,2,1:T(8,128)(2,1)}), bf16[128,4,20]{0,2,1:T(8,128)(2,1)S(1)}, u32[]{:S(2)}, u32[]{:S(2)}) async-start(bf16[128,4,20]{0,2,1:T(8,128)(2,1)} %all_to_all.44), calls=%async_computation.2 | async-start | bytes 49152 | tf_op jit(solution)/shard_map/all_to_all | solution.py:79
  12.1 5.8 %all_gather.23 = bf16[512,128]{1,0:T(8,128)(2,1)S(1)} all-gather(bf16[128,128]{1,0:T(8,128)(2,1)} %param.15), channel_id=1, replica_groups=mesh['ctx'=8,'grp'=4] {'grp'}, dimensions={0}, use_global_device_ids=true | all-gather | bytes 163840 | tf_op jit(solution)/shard_map/all_gather | solution.py:82
  17.9 2.4 %copy.51 = bf16[128,5120]{0,1:T(8,128)(2,1)} copy(bf16[128,5120]{1,0:T(8,128)(2,1)} %param.13) | data formatting | bytes 2621440 | tf_op args[0]
  20.3 0.6 all_to_all.42
  20.9 3.3 %all-to-all-start.1 = ((bf16[128,4,20]{0,2,1:T(8,128)(2,1)}), bf16[128,4,20]{0,2,1:T(8,128)(2,1)S(1)}, u32[]{:S(2)}, u32[]{:S(2)}) async-start(bf16[128,4,20]{0,2,1:T(8,128)(2,1)} %all_to_all.42), calls=%async_computation.1 | async-start | bytes 49152 | tf_op jit(solution)/shard_map/all_to_all | solution.py:78
  24.3 1.2 reduce-window.6
  25.5 0.2 slice_reduce_fusion
  25.7 2.3 %all-to-all-done.1 = bf16[128,4,20]{0,2,1:T(8,128)(2,1)S(1)} async-done(((bf16[128,4,20]{0,2,1:T(8,128)(2,1)}), bf16[128,4,20]{0,2,1:T(8,128)(2,1)S(1)}, u32[]{:S(2)}, u32[]{:S(2)}) %all-to-all-start.1) | async-done | bytes 20512 | tf_op jit(solution)/shard_map/all_to_all | solution.py:78
  28.1 3.5 %all-to-all-start = ((bf16[128,4,1280]{0,2,1:T(8,128)(2,1)}), bf16[128,4,1280]{0,2,1:T(8,128)(2,1)S(1)}, u32[]{:S(2)}, u32[]{:S(2)}) async-start(bf16[128,4,1280]{0,2,1:T(8,128)(2,1)} %bitcast), calls=%async_computation | async-start | bytes 2621440 | tf_op jit(solution)/shard_map/all_to_all | solution.py:76
  32.0 0.1 copy.60
  32.1 0.3 slice_subtract_fusion
  32.4 0.1 copy.65
  32.5 0.1 copy.66
  32.6 0.1 copy.61
  32.8 0.7 exponential_bitcast_fusion
  33.5 15.3 %all-to-all-done = bf16[128,4,1280]{0,2,1:T(8,128)(2,1)S(1)} async-done(((bf16[128,4,1280]{0,2,1:T(8,128)(2,1)}), bf16[128,4,1280]{0,2,1:T(8,128)(2,1)S(1)}, u32[]{:S(2)}, u32[]{:S(2)}) %all-to-all-start) | async-done | bytes 1310752 | tf_op jit(solution)/shard_map/all_to_all | solution.py:76
  48.8 0.2 convert_bitcast_fusion.1
  49.0 5.4 %copy.52 = f32[4,128,1280]{1,0,2:T(4,128)S(1)} copy(f32[4,128,1280]{1,2,0:T(8,128)S(1)} %convert_bitcast_fusion.1) | data formatting | bytes 5242880 | tf_op jit(solution)/shard_map/convert_element_type | solution.py:33
  54.5 3.3 %reshape.126 = f32[2,256,20,64]{1,0,3,2:T(2,128)} reshape(f32[4,128,1280]{1,0,2:T(4,128)S(1)} %copy.52) | data formatting | bytes 5242880 | tf_op jit(solution)/shard_map/convert_element_type | solution.py:33
  57.8 5.1 %broadcast_multiply_fusion = (f32[2,256,20,64]{1,0,3,2:T(2,128)S(1)}, f32[2,256,20,64]{1,0,3,2:T(2,128)}) fusion(f32[2,256,20]{1,0,2:T(2,128)S(1)} %get-tuple-element.189, f32[2,256,20,64]{1,0,3,2:T(2,128)} %reshape.126, f32[2,256,20]{1,0,2:T(2,128)S(1)} %reshape.127), kind=kLoop, calls=%fused_computation.39 | loop fusion | flops 1310720 | bytes 7946240 | tf_op jit(solution)/shard_map/mul | solution.py:50
  62.9 2.4 %fusion.22 = f32[2,20,64,128]{3,2,1,0:T(8,128)} fusion(bf16[2,256,128,1]{2,1,3,0:T(8,128)(2,1)S(1)} %bitcast.132, f32[2,256,20,64]{1,0,3,2:T(2,128)S(1)} %get-tuple-element.186), kind=kOutput, calls=%fused_computation.33 | convolution fusion | flops 1006632960 | bytes 4063232 | tf_op jit(solution)/shard_map/qjhp,qjn->qhpn/dot_general | solution.py:49
  65.3 4.3 %while.27 = (s32[]{:T(128)}, f32[20,64,128]{2,1,0:T(8,128)S(1)}, f32[2,20,64,128]{3,2,1,0:T(8,128)}, f32[2,20]{1,0:T(2,128)S(1)}, f32[2,20,64,128]{3,2,1,0:T(8,128)}, /*index=5*/s32[]{:T(128)}, s32[]{:T(128)}) while((s32[]{:T(128)}, f32[20,64,128]{2,1,0:T(8,128)S(1)}, f32[2,20,64,128]{3,2,1,0:T(8,128)}, f32[2,20]{1,0:T(2,128)S(1)}, ...), condition=%wide.region_3.4_spmd.clone, body=%wide.region_2.3_spmd.clone.sunk | while | flops 655363 | bytes 3277648 | solution.py:58
  65.3 0.9 bitcast_dynamic-update-slice_fusion.2
  66.2 1.2 bitcast_add_fusion.3
  67.5 0.9 bitcast_dynamic-update-slice_fusion.2
  68.4 1.2 bitcast_add_fusion.3
  69.6 0.8 copy-done
  70.5 2.5 %copy.68 = bf16[128,5120]{0,1:T(8,128)(2,1)} copy(bf16[128,5120]{1,0:T(8,128)(2,1)} %param.14) | data formatting | bytes 2621440 | tf_op args[1]
  72.9 4.3 %all-to-all-start.3 = ((bf16[128,4,1280]{0,2,1:T(8,128)(2,1)}), bf16[128,4,1280]{0,2,1:T(8,128)(2,1)}, u32[]{:S(2)}, u32[]{:S(2)}) async-start(bf16[128,4,1280]{0,2,1:T(8,128)(2,1)} %bitcast.128), calls=%async_computation.3 | async-start | bytes 2621440 | tf_op jit(solution)/shard_map/all_to_all | solution.py:77
  77.4 0.6 dynamic-slice
  78.5 17.5 %all_gather.22 = bf16[512,128]{1,0:T(8,128)(2,1)S(1)} all-gather(bf16[128,128]{1,0:T(8,128)(2,1)} %param.16), channel_id=1, replica_groups=mesh['ctx'=8,'grp'=4] {'grp'}, dimensions={0}, use_global_device_ids=true | all-gather | bytes 163840 | tf_op jit(solution)/shard_map/all_gather | solution.py:83
  96.0 0.6 iota_compare_fusion
  96.7 1.0 fusion.28
  97.7 1.4 copy.57
  99.1 0.8 copy.63
  99.9 0.1 exponential_dynamic-update-slice_fusion
  100.0 22.7 %all-reduce = f32[160]{0:T(256)S(1)} all-reduce(f32[160]{0:T(256)S(1)} %exponential_dynamic-update-slice_fusion), channel_id=2, replica_groups=mesh['ctx'=8,'grp'=4] {'ctx'}, use_global_device_ids=true, to_apply=%add | all-reduce | flops 160 | bytes 1280
  122.7 0.1 reshape.133
  122.8 0.8 pad
  123.6 0.6 copy.75
  124.2 2.1 reshape.129
  126.3 13.1 %fusion.2 = f32[2,20,64,256]{3,2,1,0:T(8,128)S(1)} fusion(f32[2,256,256]{2,1,0:T(8,128)} %fusion.28, f32[2,20,256]{2,1,0:T(8,128)} %copy.57, pred[256,256]{1,0:T(8,128)(4,1)S(1)} %copy-done.3, f32[2,256,20,64]{1,0,3,2:T(2,128)} %get-tuple-element.187), kind=kOutput, calls=%fused_computation.7 | convolution fusion | flops 2021130240 | bytes 5873664 | tf_op jit(solution)/shard_map/qhij,qjhp->qihp/dot_general | solution.py:45
  139.5 1.3 fusion.21
  140.9 1.9 copy.74
  142.7 1.6 copy.69
  144.3 1.7 convert_bitcast_fusion
  146.1 4.1 %copy.71 = f32[4,128,1280]{1,0,2:T(4,128)} copy(f32[4,128,1280]{2,1,0:T(8,128)} %convert_bitcast_fusion) | data formatting | bytes 5242880 | tf_op jit(solution)/shard_map/convert_element_type | solution.py:104
  150.2 4.1 %reshape.131 = f32[512,20,64]{0,2,1:T(8,128)} reshape(f32[4,128,1280]{1,0,2:T(4,128)} %copy.71) | data formatting | bytes 5242880 | tf_op jit(solution)/shard_map/convert_element_type | solution.py:104
  154.4 3.5 %all-gather.6.cloned.1.call-done = f32[160,64,128]{2,1,0:T(8,128)} async-done(((f32[20,64,128]{2,1,0:T(8,128)}), f32[160,64,128]{2,1,0:T(8,128)}) %all-gather.6.cloned.1.call-update) | async-done | bytes 5242896 | tf_op jit(solution)/shard_map/all_gather | solution.py:14
  157.9 8.9 %while.28 = (s32[]{:T(128)}, f32[20,64,128]{2,1,0:T(8,128)S(1)}, s32[]{:T(128)}, f32[8,20]{1,0:T(8,128)S(1)}, f32[8,20,64,128]{3,2,1,0:T(8,128)}, /*index=5*/s32[]{:T(128)}, s32[]{:T(128)}) while((s32[]{:T(128)}, f32[20,64,128]{2,1,0:T(8,128)S(1)}, s32[]{:T(128)}, f32[8,20]{1,0:T(8,128)S(1)}, f32[8,20,64,128]{3,2,1,0:T(8,128)}, ...), condition=%wide.region_6.7_spmd.clone, body=%wide.region_5.6_spmd.clone.sunk | while | flops 655364 | bytes 1966425 | solution.py:23
  157.9 1.2 fusion.40
  159.2 1.2 fusion.40
  160.5 1.2 fusion.40
  161.7 1.2 fusion.40
  163.0 1.2 fusion.40
  164.3 1.2 fusion.40
  165.6 1.2 fusion.40
  166.8 6.9 %multiply_reduce_fusion = (f32[512]{0:T(512)S(1)}, f32[512,20,64]{0,2,1:T(8,128)}) fusion(f32[512,20,64]{0,2,1:T(8,128)} %reshape.131, f32[512,20,64]{0,2,1:T(8,128)} %reshape.129, f32[20]{0:T(128)S(1)} %copy-done.7, f32[512,20,64]{0,2,1:T(8,128)} %bitcast.129, f32[512,20]{0,1:T(8,128)S(1)} %bitcast.140, f32[20,64,128]{2,1,0:T(8,128)S(1)} %get-tuple-element.129, ...), kind=kOutput, calls=%fused_computation.37 | convolution fusion | flops 1013841408 | bytes 11315280 | tf_op jit(solution)/shard_map/tn,hpn->thp/dot_general | solution.py:99
  173.7 3.2 %copy.70 = f32[512,1280]{1,0:T(8,128)} copy(f32[512,1280]{0,1:T(8,128)} %bitcast.130) | data formatting | bytes 5242880 | tf_op jit(solution)/shard_map/reshape | solution.py:103
  176.9 5.4 %all-gather.3 = f32[4,1,512]{2,1,0:T(1,128)S(1)} all-gather(f32[1,1,512]{2,1,0:T(1,128)S(1)} %bitcast.143), channel_id=4, replica_groups=mesh['ctx'=8,'grp'=4] {'grp'}, dimensions={0}, use_global_device_ids=true | all-gather | bytes 10240 | tf_op jit(solution)/shard_map/all_gather | solution.py:106
  182.4 2.6 %fusion.25 = bf16[512,1280]{1,0:T(8,128)(2,1)S(1)} fusion(f32[512,1280]{1,0:T(8,128)} %copy.70, bf16[128,4,1280]{2,0,1:T(8,128)(2,1)S(1)} %copy.69, f32[1280]{0:T(1024)S(1)} %copy-done.6, f32[512]{0:T(512)S(1)} %add_rsqrt_fusion), kind=kLoop, calls=%fused_computation.38 | loop fusion | flops 5898240 | bytes 5250048 | tf_op jit(solution)/shard_map/convert_element_type | solution.py:108
  185.0 7.7 %convolution_convert_fusion = bf16[512,2560]{1,0:T(8,128)(2,1)} fusion(bf16[512,1280]{1,0:T(8,128)(2,1)S(1)} %fusion.25, bf16[1280,2560]{1,0:T(8,128)(2,1)} %param.21), kind=kOutput, calls=%fused_computation.17 | convolution fusion | flops 3356753920 | bytes 10485760 | tf_op jit(solution)/shard_map/dot_general | solution.py:110
  192.7 33.0 %reduce-scatter.2.cloned.1.call-done = bf16[128,2560]{1,0:T(8,128)(2,1)} async-done(((bf16[512,2560]{1,0:T(8,128)(2,1)}), bf16[128,2560]{1,0:T(8,128)(2,1)}) %reduce-scatter.2.cloned.1.call-update) | async-done | bytes 655376 | tf_op jit(solution)/shard_map/reduce_scatter | solution.py:109
  (54 shorter events, 0.8 us)
Async XLA Ops:
  6.5 13.8 %copy-start.5 = (bf16[128,80]{0,1:T(8,128)(2,1)S(1)}, bf16[128,80]{0,1:T(8,128)(2,1)}, u32[]{:S(2)}) copy-start(bf16[128,80]{0,1:T(8,128)(2,1)} %param.17) | copy-start | bytes 61444
  7.9 13.0 %all-to-all-start.2 = ((bf16[128,4,20]{0,2,1:T(8,128)(2,1)}), bf16[128,4,20]{0,2,1:T(8,128)(2,1)S(1)}, u32[]{:S(2)}, u32[]{:S(2)}) async-start(bf16[128,4,20]{0,2,1:T(8,128)(2,1)} %all_to_all.44), calls=%async_computation.2 | async-start | bytes 49152 | tf_op jit(solution)/shard_map/all_to_all | solution.py:79
  20.9 7.1 %all-to-all-start.1 = ((bf16[128,4,20]{0,2,1:T(8,128)(2,1)}), bf16[128,4,20]{0,2,1:T(8,128)(2,1)S(1)}, u32[]{:S(2)}, u32[]{:S(2)}) async-start(bf16[128,4,20]{0,2,1:T(8,128)(2,1)} %all_to_all.42), calls=%async_computation.1 | async-start | bytes 49152 | tf_op jit(solution)/shard_map/all_to_all | solution.py:78
  28.1 20.8 %all-to-all-start = ((bf16[128,4,1280]{0,2,1:T(8,128)(2,1)}), bf16[128,4,1280]{0,2,1:T(8,128)(2,1)S(1)}, u32[]{:S(2)}, u32[]{:S(2)}) async-start(bf16[128,4,1280]{0,2,1:T(8,128)(2,1)} %bitcast), calls=%async_computation | async-start | bytes 2621440 | tf_op jit(solution)/shard_map/all_to_all | solution.py:76
  31.6 126.3 %all-gather.6.cloned.1.call-start = ((), (), s32[]{:S(2)}) async-start(), calls=%async_computation.6 | async-start | bytes 5898240 | tf_op jit(solution)/shard_map/all_gather | solution.py:14
  31.8 17.0 %copy-start.2 = (f32[2,20,256]{2,0,1:T(2,128)}, f32[2,20,256]{2,0,1:T(2,128)S(1)}, u32[]{:S(2)}) copy-start(f32[2,20,256]{2,0,1:T(2,128)S(1)} %reduce_window_sum.35) | copy-start | bytes 122884
  69.6 0.8 copy-start
  70.5 6.9 %copy-start.8 = (u32[32]{0:T(128)S(1)}, u32[32]{0:T(128)}, u32[]{:S(2)}) copy-start(u32[32]{0:T(128)} %constant.61) | copy-start | bytes 388
  72.9 69.8 %all-to-all-start.3 = ((bf16[128,4,1280]{0,2,1:T(8,128)(2,1)}), bf16[128,4,1280]{0,2,1:T(8,128)(2,1)}, u32[]{:S(2)}, u32[]{:S(2)}) async-start(bf16[128,4,1280]{0,2,1:T(8,128)(2,1)} %bitcast.128), calls=%async_computation.3 | async-start | bytes 2621440 | tf_op jit(solution)/shard_map/all_to_all | solution.py:77
  77.3 148.5 %reduce-scatter.2.cloned.1.call-start = ((), (), s32[]{:S(2)}) async-start(), calls=%async_computation.5 | async-start | bytes 3276800 | tf_op jit(solution)/shard_map/reduce_scatter | solution.py:109
  124.2 2.1 copy-start.3
  126.3 13.1 %copy-start.1 = (f32[2,20,64,128]{3,2,1,0:T(8,128)S(1)}, f32[2,20,64,128]{3,2,1,0:T(8,128)}, u32[]{:S(2)}) copy-start(f32[2,20,64,128]{3,2,1,0:T(8,128)} %get-tuple-element.127) | copy-start | bytes 3932164
  157.9 8.9 %copy-start.4 = (f32[3,8,2,256]{3,1,2,0:T(8,128)S(1)}, f32[3,8,2,256]{3,1,2,0:T(8,128)}, u32[]{:S(2)}) copy-start(f32[3,8,2,256]{3,1,2,0:T(8,128)} %copy.75) | copy-start | bytes 147460
  157.9 8.9 %copy-start.7 = (f32[20]{0:T(128)S(1)}, f32[20]{0:T(128)}, u32[]{:S(2)}) copy-start(f32[20]{0:T(128)} %param.19) | copy-start | bytes 244
  173.7 8.7 %copy-start.6 = (f32[1280]{0:T(1024)S(1)}, f32[1280]{0:T(1024)}, u32[]{:S(2)}) copy-start(f32[1280]{0:T(1024)} %param.20) | copy-start | bytes 15364
Sparse Core Ops, SparseCore 0:
  70.6 87.2 all-gather.5
  192.8 32.8 reduce-scatter.1
